TPU v7x, 256 devices: a whole 4x4x8 slice. The times are simulated.
256 devices in a mesh: tensor: 4 (over x), shard: 64 (over z, y, core).
Axes of the slice: x: 4, y: 4, z: 8, core: 2. Of those that a mesh axis runs over, the one named last changes fastest.
Arguments:
- proj_grads: bfloat16 [128, 2, 1152, 1024], P('shard', None, None, 'tensor'), may hold values from -60 to 60
- kv_grads: bfloat16 [512, 1152, 512], P(('tensor', 'shard')), may hold values from -60 to 60
- gain_grads: bfloat16 [512, 2, 256], P(('tensor', 'shard')), may hold values from -60 to 60
- proj_master: float32 [2, 1152, 1024], P(None, 'shard', 'tensor'), may hold values from -0.3125 to 0.3125
- proj_m: float32 [2, 1152, 1024], P(None, 'shard', 'tensor'), may hold values from -1.5 to 1.5
- proj_v: float32 [2, 1152, 1024], P(None, 'shard', 'tensor'), may hold values from 0.02 to 0.5
- kv_master: float32 [1152, 512], P('shard', 'tensor'), may hold values from -0.3125 to 0.3125
- kv_m: float32 [1152, 512], P('shard', 'tensor'), may hold values from -1.5 to 1.5
- kv_v: float32 [1152, 512], P('shard', 'tensor'), may hold values from 0.02 to 0.5
- gains: float32 [2, 256], replicated, may hold values from 0.1 to 1.9
- gains_m: float32 [2, 256], replicated, may hold values from -6 to 6
- gains_v: float32 [2, 256], replicated, may hold values from 0.25 to 4
Outputs:
- proj_master_new: float32 [2, 1152, 1024], P(None, 'shard', 'tensor')
- proj_m_new: float32 [2, 1152, 1024], P(None, 'shard', 'tensor')
- proj_v_new: float32 [2, 1152, 1024], P(None, 'shard', 'tensor')
- proj_weights: bfloat16 [2, 1152, 1024], P(None, None, 'tensor')
- kv_master_new: float32 [1152, 512], P('shard', 'tensor')
- kv_m_new: float32 [1152, 512], P('shard', 'tensor')
- kv_v_new: float32 [1152, 512], P('shard', 'tensor')
- kv_weights: bfloat16 [1152, 512], replicated
- gains_new: float32 [2, 256], replicated
- gains_m_new: float32 [2, 256], replicated
- gains_v_new: float32 [2, 256], replicated
All inputs are finite; a program needn't handle non-finite values.
Results may differ from a plain program's by a relative error of at most 0.0004.
Values may be sent and summed in bfloat16 or wider, within the bound.
A program may use at most 64 MiB of HBM per device.

v0:
```python
import math
import jax
import jax.numpy as jnp
from jax import lax
from jax.sharding import PartitionSpec as P

PARAMS = 2949632
beta_one = 0.9
beta_two = 0.95
learn_rate = 0.01
decay_rate = 0.1
epsilon = 1e-08
step_count = 10


def adamw_step(master, moment, second, update_grad, decay):
    moment_new = beta_one * moment + (1.0 - beta_one) * update_grad
    second_new = beta_two * second + (1.0 - beta_two) * update_grad * update_grad
    first_hat = moment_new / (1.0 - beta_one**step_count)
    second_hat = second_new / (1.0 - beta_two**step_count)
    master_new = master - learn_rate * (
        first_hat / (jnp.sqrt(second_hat) + epsilon) + decay * master
    )
    return (master_new, moment_new, second_new)


def shards(
    proj_grads,
    kv_grads,
    gain_grads,
    proj_master,
    proj_m,
    proj_v,
    kv_master,
    kv_m,
    kv_v,
    gains,
    gains_m,
    gains_v,
):
    proj_local = jnp.sum(proj_grads, axis=0, dtype=jnp.float32)
    kv_local = jnp.sum(kv_grads, axis=0, dtype=jnp.float32)
    gain_local = jnp.sum(gain_grads, axis=0, dtype=jnp.float32)
    gain_sum = lax.psum(gain_local, ("tensor", "shard"))
    proj_owned, kv_row_part = (
        lax.psum_scatter(proj_local, "shard", scatter_dimension=1, tiled=True),
        lax.psum_scatter(kv_local, "shard", scatter_dimension=0, tiled=True),
    )
    kv_owned = lax.psum_scatter(kv_row_part, "tensor", scatter_dimension=1, tiled=True)
    owned_square = jnp.sum(proj_owned * proj_owned) + jnp.sum(kv_owned * kv_owned)
    norm_square = lax.psum(owned_square, ("tensor", "shard")) + jnp.sum(gain_sum * gain_sum)
    clip_factor = jnp.minimum(1.0, math.sqrt(PARAMS) / jnp.sqrt(norm_square))
    proj_new, proj_m_new, proj_v_new = adamw_step(
        proj_master, proj_m, proj_v, clip_factor * proj_owned, decay_rate
    )
    kv_new, kv_m_new, kv_v_new = adamw_step(
        kv_master, kv_m, kv_v, clip_factor * kv_owned, decay_rate
    )
    gains_new, gains_m_new, gains_v_new = adamw_step(
        gains, gains_m, gains_v, clip_factor * gain_sum, 0.0
    )
    proj_half = proj_new.astype(jnp.bfloat16)
    kv_half = kv_new.astype(jnp.bfloat16)
    kv_wide = lax.all_gather(kv_half, "tensor", axis=1, tiled=True)
    proj_weights, kv_weights = (
        lax.all_gather(proj_half, "shard", axis=1, tiled=True),
        lax.all_gather(kv_wide, "shard", axis=0, tiled=True),
    )
    return (
        proj_new,
        proj_m_new,
        proj_v_new,
        proj_weights,
        kv_new,
        kv_m_new,
        kv_v_new,
        kv_weights,
        gains_new,
        gains_m_new,
        gains_v_new,
    )


def solution(mesh):
    placed = (
        P("shard", None, None, "tensor"),
        P(("tensor", "shard"), None, None),
        P(("tensor", "shard"), None, None),
        P(None, "shard", "tensor"),
        P(None, "shard", "tensor"),
        P(None, "shard", "tensor"),
        P("shard", "tensor"),
        P("shard", "tensor"),
        P("shard", "tensor"),
        P(),
        P(),
        P(),
    )
    return jax.shard_map(
        shards,
        mesh=mesh,
        in_specs=placed,
        out_specs=(
            P(None, "shard", "tensor"),
            P(None, "shard", "tensor"),
            P(None, "shard", "tensor"),
            P(None, None, "tensor"),
            P("shard", "tensor"),
            P("shard", "tensor"),
            P("shard", "tensor"),
            P(),
            P(),
            P(),
            P(),
        ),
        check_vma=False,
    )
```

profile of v0, /device:TPU:1, one launch (start us, length us, event | category | flops | bytes accessed | tf_op | source)
XLA Modules:
  0.0 487.7 jit_solution(7765557723649341525)
XLA Ops:
  7.2 0.0 all-reduce.6.cloned.1.call-start
  7.2 2.3 convert_reduce_fusion.1
  9.5 0.0 copy-start
  9.5 7.6 %copy.25 = f32[2,1152,256]{2,0,1:T(2,128)} copy(f32[2,1152,256]{2,1,0:T(8,128)S(1)} %convert_reduce_fusion.1) | data formatting | bytes 4718592 | tf_op jit(solution)/shard_map/reduce_sum | solution.py:41
  17.2 0.0 copy-done
  17.2 2.0 convert_reduce_fusion
  19.2 0.0 copy-start.11
  19.2 0.0 copy-start.7
  19.2 0.0 copy-start.1
  19.2 0.0 copy-start.2
  19.2 0.0 copy-start.3
  19.2 0.0 copy-start.4
  19.2 0.0 copy-start.5
  19.2 0.0 copy-start.6
  19.2 0.0 copy-start.8
  19.2 0.0 copy-start.9
  19.3 0.0 copy-start.10
  19.3 0.0 all-reduce.6.cloned.1.call-update
  19.3 0.0 reduce-scatter.2.cloned.1.call-start
  19.3 0.5 copy-done.11
  19.9 0.6 dynamic-slice
  21.1 197.5 %all-reduce.6.cloned.1.call-done = (f32[2,1152,256]{2,0,1:T(2,128)}, f32[1152,512]{1,0:T(8,128)}) async-done(((f32[2,1152,256]{2,0,1:T(2,128)}, f32[1152,512]{1,0:T(8,128)}), (f32[2,1152,256]{2,0,1:T(2,128)}, f32[1152,512]{1,0:T(8,128)})) %all-reduce.6.cloned.1.call-update) | async-done | bytes 4718608
  218.6 1.5 constant_dynamic-slice_fusion
  220.1 0.0 reduce-scatter.2.cloned.1.call-update
  220.1 0.0 all-gather.4.cloned.1.call-start
  220.1 0.0 copy-done.7
  220.2 1.4 multiply_reduce_fusion
  221.6 21.1 %reduce-scatter.2.cloned.1.call-done = f32[18,128]{1,0:T(8,128)} async-done(((f32[18,512]{1,0:T(8,128)}), f32[18,128]{1,0:T(8,128)}) %reduce-scatter.2.cloned.1.call-update) | async-done | bytes 9232 | tf_op jit(solution)/shard_map/reduce_scatter | solution.py:49
  242.7 1.3 multiply_reduce_fusion.1
  245.3 78.1 %all-reduce.2 = (f32[]{:T(128)}, f32[2,256]{1,0:T(2,128)S(1)}) all-reduce(f32[]{:T(128)S(6)} %add.61, f32[2,256]{1,0:T(2,128)S(1)} %convert_reduce_fusion.2), channel_id=1, replica_groups=mesh['tensor'=4,'shard'=64] {'tensor','shard'}, use_global_device_ids=true, to_apply=%region_7.0 | all-reduce | flops 513 | bytes 4104 | tf_op jit(solution)/shard_map/psum | solution.py:51
  323.5 0.6 multiply_reduce_fusion.2
  325.4 0.0 copy-done.1
  325.4 0.0 copy-done.2
  325.4 0.0 copy-done.3
  325.4 1.5 fusion.6
  327.0 0.0 all-gather.4.cloned.1.call-update
  327.0 0.0 all-gather.6.cloned.1.call-start
  327.0 0.0 copy-done.4
  327.1 0.0 copy-done.5
  327.1 0.0 copy-done.6
  327.1 1.3 fusion.4
  328.4 8.5 %all_gather.10 = bf16[18,512]{1,0:T(8,128)(2,1)} all-gather(bf16[18,128]{1,0:T(8,128)(2,1)S(1)} %get-tuple-element.29), channel_id=1, replica_groups=mesh['tensor'=4,'shard'=64] {'tensor'}, dimensions={1}, use_global_device_ids=true | all-gather | bytes 23040 | tf_op jit(solution)/shard_map/all_gather | solution.py:64
  336.9 0.0 all-gather.6.cloned.1.call-update
  336.9 0.0 copy-done.8
  336.9 0.0 copy-done.9
  336.9 0.0 copy-done.10
  336.9 0.6 multiply_subtract_fusion.2
  337.5 63.2 %all-gather.4.cloned.1.call-done = bf16[2,1152,256]{2,0,1:T(2,128)(2,1)} async-done(((bf16[2,18,256]{2,0,1:T(2,128)(2,1)}), bf16[2,1152,256]{2,0,1:T(2,128)(2,1)}) %all-gather.4.cloned.1.call-update) | async-done | bytes 1179664 | tf_op jit(solution)/shard_map/all_gather | solution.py:66
  400.7 2.4 copy.26
  403.2 74.9 %all-gather.6.cloned.1.call-done = bf16[64,18,512]{2,1,0:T(8,128)(2,1)} async-done(((bf16[1,18,512]{2,1,0:T(8,128)(2,1)}), bf16[64,18,512]{2,1,0:T(8,128)(2,1)}) %all-gather.6.cloned.1.call-update) | async-done | bytes 1179664 | tf_op jit(solution)/shard_map/all_gather | solution.py:67
  478.1 3.1 reshape.23
  (1 shorter events, 0.0 us)
Async XLA Ops:
  7.2 211.4 %all-reduce.6.cloned.1.call-start = ((), (), s32[]{:S(2)}) async-start(), calls=%async_computation.4 | async-start | bytes 9437184
  9.5 7.7 %copy-start = (bf16[2,1152,512]{2,1,0:T(8,128)(2,1)S(1)}, bf16[2,1152,512]{2,1,0:T(8,128)(2,1)}, u32[]{:S(2)}) copy-start(bf16[2,1152,512]{2,1,0:T(8,128)(2,1)} %param.13) | copy-start | bytes 7077892
  19.2 0.7 copy-start.11
  19.2 201.0 %copy-start.7 = (bf16[2,2,256]{2,1,0:T(2,128)(2,1)S(1)}, bf16[2,2,256]{2,1,0:T(2,128)(2,1)}, u32[]{:S(2)}) copy-start(bf16[2,2,256]{2,1,0:T(2,128)(2,1)} %param.14) | copy-start | bytes 6148
  19.2 306.2 %copy-start.1 = (f32[2,18,256]{2,0,1:T(2,128)S(1)}, f32[2,18,256]{2,0,1:T(2,128)}, u32[]{:S(2)}) copy-start(f32[2,18,256]{2,0,1:T(2,128)} %param.15) | copy-start | bytes 110596
  19.2 306.2 %copy-start.2 = (f32[2,18,256]{2,0,1:T(2,128)S(1)}, f32[2,18,256]{2,0,1:T(2,128)}, u32[]{:S(2)}) copy-start(f32[2,18,256]{2,0,1:T(2,128)} %param.16) | copy-start | bytes 110596
  19.2 306.2 %copy-start.3 = (f32[2,18,256]{2,0,1:T(2,128)S(1)}, f32[2,18,256]{2,0,1:T(2,128)}, u32[]{:S(2)}) copy-start(f32[2,18,256]{2,0,1:T(2,128)} %param.17) | copy-start | bytes 110596
  19.2 307.9 %copy-start.4 = (f32[18,128]{1,0:T(8,128)S(1)}, f32[18,128]{1,0:T(8,128)}, u32[]{:S(2)}) copy-start(f32[18,128]{1,0:T(8,128)} %param.18) | copy-start | bytes 27652
  19.2 307.9 %copy-start.5 = (f32[18,128]{1,0:T(8,128)S(1)}, f32[18,128]{1,0:T(8,128)}, u32[]{:S(2)}) copy-start(f32[18,128]{1,0:T(8,128)} %param.19) | copy-start | bytes 27652
  19.2 307.9 %copy-start.6 = (f32[18,128]{1,0:T(8,128)S(1)}, f32[18,128]{1,0:T(8,128)}, u32[]{:S(2)}) copy-start(f32[18,128]{1,0:T(8,128)} %param.20) | copy-start | bytes 27652
  19.2 317.7 %copy-start.8 = (f32[2,256]{1,0:T(2,128)S(1)}, f32[2,256]{1,0:T(2,128)}, u32[]{:S(2)}) copy-start(f32[2,256]{1,0:T(2,128)} %param.21) | copy-start | bytes 6148
  19.2 317.7 %copy-start.9 = (f32[2,256]{1,0:T(2,128)S(1)}, f32[2,256]{1,0:T(2,128)}, u32[]{:S(2)}) copy-start(f32[2,256]{1,0:T(2,128)} %param.22) | copy-start | bytes 6148
  19.3 317.7 %copy-start.10 = (f32[2,256]{1,0:T(2,128)S(1)}, f32[2,256]{1,0:T(2,128)}, u32[]{:S(2)}) copy-start(f32[2,256]{1,0:T(2,128)} %param.23) | copy-start | bytes 6148
  19.3 223.4 %reduce-scatter.2.cloned.1.call-start = ((), (), s32[]{:S(2)}) async-start(), calls=%async_computation.1 | async-start | bytes 61440 | tf_op jit(solution)/shard_map/reduce_scatter | solution.py:49
  220.1 180.6 %all-gather.4.cloned.1.call-start = ((), (), s32[]{:S(2)}) async-start(), calls=%async_computation.2 | async-start | bytes 1198080 | tf_op jit(solution)/shard_map/all_gather | solution.py:66
  327.0 151.1 %all-gather.6.cloned.1.call-start = ((), (), s32[]{:S(2)}) async-start(), calls=%async_computation.3 | async-start | bytes 1597440 | tf_op jit(solution)/shard_map/all_gather | solution.py:67
Sparse Core Ops, SparseCore 0:
  19.4 199.1 all-reduce.5
  221.8 20.8 reduce-scatter.1
  327.1 73.5 all-gather.3
  403.4 74.6 all-gather.5
where the time goes:
time: 488 us
  waiting for transfers between devices  357 us (73%)
  blocking collectives  86.6 us (18%)
  between operations  17.2 us (4%)
  local copies, waits for them, and re-layouts  15.8 us (3%)
  other arithmetic  11.1 us (2%)
    unnamed x5, waiting for transfers between devices  198 us
    psum x1, blocking collectives, shards(): lax.psum(owned_square, ('tensor', 'shard')) + jnp.sum(gain_sum * gain_sum)  78.1 us
    all_gather x1, waiting for transfers between devices, shards(): lax.all_gather(kv_wide, 'shard', axis=0, tiled=True)  74.9 us
    all_gather x1, waiting for transfers between devices, shards(): lax.all_gather(proj_half, 'shard', axis=1, tiled=True)  63.2 us
    reduce_scatter x1, waiting for transfers between devices, shards(): lax.psum_scatter(kv_row_part, 'tensor', scatter_dimension=1, tiled=True)  21.1 us
  transfers between devices with their start and end apart: 4, of which 4 were waited for; matrix products, arithmetic and copies ran while one was open for 1% of the time, Pallas kernels for 0%

commit v1 on v0

--- a/solution.py
+++ b/solution.py
@@ -3,6 +3,7 @@
 import jax.numpy as jnp
 from jax import lax
 from jax.sharding import PartitionSpec as P
+from jax.lax import all_to_all, axis_size
 
 PARAMS = 2949632
 beta_one = 0.9
@@ -63,7 +64,15 @@
     kv_half = kv_new.astype(jnp.bfloat16)
     kv_wide = lax.all_gather(kv_half, "tensor", axis=1, tiled=True)
     proj_weights, kv_weights = (
-        lax.all_gather(proj_half, "shard", axis=1, tiled=True),
+        jnp.concatenate(
+            all_to_all(
+                jnp.stack(axis_size("shard") * [proj_half]),
+                axis_name="shard",
+                split_axis=0,
+                concat_axis=0,
+            ),
+            axis=1,
+        ),
         lax.all_gather(kv_wide, "shard", axis=0, tiled=True),
     )
     return (

time: 488 us -> 436 us (0.89)
  waiting for transfers between devices: 357 us -> 297 us
  starting transfers between devices: 0.16 us -> 7.72 us
    all_gather x1 -> x0, waiting for transfers between devices: 63.2 us -> none  [shards(): lax.all_gather(proj_half, 'shard', axis=1, tiled=True)]
    all_to_all x0 -> x1, waiting for transfers between devices: none -> 20.2 us  [shards(): all_to_all(jnp.stack(axis_size('shard') * [proj_half]), axis_name='shard'...]
    all_gather x1, waiting for transfers between devices: 74.9 us -> 57.9 us  [shards(): lax.all_gather(kv_wide, 'shard', axis=0, tiled=True)]
    all_to_all x0 -> x1, starting transfers between devices: none -> 7.6 us  [shards(): all_to_all(jnp.stack(axis_size('shard') * [proj_half]), axis_name='shard'...]
    unnamed x5 -> x4, waiting for transfers between devices: 198 us -> 197 us
where the time goes in v1:
time: 436 us
  waiting for transfers between devices  297 us (68%)
  blocking collectives  87.1 us (20%)
  between operations  17.2 us (4%)
  local copies, waits for them, and re-layouts  16.1 us (4%)
  other arithmetic  10.5 us (2%)
  starting transfers between devices  7.72 us (2%)
    unnamed x4, waiting for transfers between devices  197 us
    psum x1, blocking collectives, shards(): lax.psum(owned_square, ('tensor', 'shard')) + jnp.sum(gain_sum * gain_sum)  78.1 us
    all_gather x1, waiting for transfers between devices, shards(): lax.all_gather(kv_wide, 'shard', axis=0, tiled=True)  57.9 us
    reduce_scatter x1, waiting for transfers between devices, shards(): lax.psum_scatter(kv_row_part, 'tensor', scatter_dimension=1, tiled=True)  21.2 us
    all_to_all x1, waiting for transfers between devices, shards(): all_to_all(jnp.stack(axis_size('shard') * [proj_half]), axis_name='shard'...  20.2 us
    all_gather x1, blocking collectives, shards(): kv_wide = lax.all_gather(kv_half, 'tensor', axis=1, tiled=True)  9.01 us
  transfers between devices with their start and end apart: 4, of which 4 were waited for; matrix products, arithmetic and copies ran while one was open for 1% of the time, Pallas kernels for 0%

profile of v1, /device:TPU:1, one launch (start us, length us, event | category | flops | bytes accessed | tf_op | source)
XLA Modules:
  0.0 435.5 jit_solution(13094088748155352786)
XLA Ops:
  7.2 0.0 all-reduce.6.cloned.1.call-start
  7.2 2.3 convert_reduce_fusion.1
  9.6 0.0 copy-start
  9.6 7.6 %copy.25 = f32[2,1152,256]{2,0,1:T(2,128)} copy(f32[2,1152,256]{2,1,0:T(8,128)S(1)} %convert_reduce_fusion.1) | data formatting | bytes 4718592 | tf_op jit(solution)/shard_map/reduce_sum | solution.py:42
  17.2 0.0 copy-done
  17.2 2.0 convert_reduce_fusion
  19.2 0.0 copy-start.12
  19.2 0.0 copy-start.8
  19.2 0.0 copy-start.2
  19.2 0.0 copy-start.3
  19.2 0.0 copy-start.4
  19.2 0.0 all-reduce.6.cloned.1.call-update
  19.3 0.0 copy-start.5
  19.3 0.0 copy-start.6
  19.3 0.0 copy-start.7
  19.3 0.0 copy-start.9
  19.3 0.0 copy-start.10
  19.3 0.0 copy-start.11
  19.3 0.0 reduce-scatter.2.cloned.1.call-start
  19.4 0.5 copy-done.12
  19.9 0.6 dynamic-slice
  21.1 197.4 %all-reduce.6.cloned.1.call-done = (f32[2,1152,256]{2,0,1:T(2,128)}, f32[1152,512]{1,0:T(8,128)}) async-done(((f32[2,1152,256]{2,0,1:T(2,128)}, f32[1152,512]{1,0:T(8,128)}), (f32[2,1152,256]{2,0,1:T(2,128)}, f32[1152,512]{1,0:T(8,128)})) %all-reduce.6.cloned.1.call-update) | async-done | bytes 4718608
  218.6 1.5 constant_dynamic-slice_fusion
  220.0 0.0 reduce-scatter.2.cloned.1.call-update
  220.1 0.0 copy-done.8
  220.1 1.4 multiply_reduce_fusion
  221.5 21.2 %reduce-scatter.2.cloned.1.call-done = f32[18,128]{1,0:T(8,128)} async-done(((f32[18,512]{1,0:T(8,128)}), f32[18,128]{1,0:T(8,128)}) %reduce-scatter.2.cloned.1.call-update) | async-done | bytes 9232 | tf_op jit(solution)/shard_map/reduce_scatter | solution.py:50
  242.7 0.0 copy-start.1
  242.7 1.4 multiply_reduce_fusion.1
  245.4 78.1 %all-reduce.2 = (f32[]{:T(128)}, f32[2,256]{1,0:T(2,128)S(1)}) all-reduce(f32[]{:T(128)S(6)} %add.61, f32[2,256]{1,0:T(2,128)S(1)} %convert_reduce_fusion.2), channel_id=1, replica_groups=mesh['tensor'=4,'shard'=64] {'tensor','shard'}, use_global_device_ids=true, to_apply=%region_7.0 | all-reduce | flops 513 | bytes 4104 | tf_op jit(solution)/shard_map/psum | solution.py:52
  323.5 0.6 multiply_reduce_fusion.2
  325.4 0.0 copy-done.2
  325.5 0.0 copy-done.3
  325.5 0.0 copy-done.4
  325.5 1.5 fusion.6
  327.0 1.6 stack.2
  328.6 7.6 %all-to-all-start = ((bf16[64,2,18,256]{3,1,2,0:T(2,128)(2,1)}), bf16[64,2,18,256]{3,1,2,0:T(2,128)(2,1)S(1)}, u32[]{:S(2)}, u32[]{:S(2)}) async-start(bf16[64,2,18,256]{3,1,2,0:T(2,128)(2,1)} %stack.2), calls=%async_computation.1 | async-start | bytes 2359296 | tf_op jit(solution)/shard_map/all_to_all | solution.py:68
  336.2 0.0 all-gather.3.cloned.1.call-start
  336.3 0.0 copy-done.5
  336.3 0.0 copy-done.6
  336.3 0.0 copy-done.7
  336.3 0.0 copy-done.1
  336.3 0.6 fusion.4
  337.0 9.0 %all_gather.6 = bf16[18,512]{1,0:T(8,128)(2,1)} all-gather(bf16[18,128]{1,0:T(8,128)(2,1)S(1)} %get-tuple-element.40), channel_id=1, replica_groups=mesh['tensor'=4,'shard'=64] {'tensor'}, dimensions={1}, use_global_device_ids=true | all-gather | bytes 23040 | tf_op jit(solution)/shard_map/all_gather | solution.py:65
  346.0 0.0 all-gather.3.cloned.1.call-update
  346.0 0.0 copy-done.9
  346.0 0.0 copy-done.10
  346.0 0.0 copy-done.11
  346.0 0.6 multiply_subtract_fusion.2
  346.6 20.2 %all-to-all-done = bf16[64,2,18,256]{3,1,2,0:T(2,128)(2,1)S(1)} async-done(((bf16[64,2,18,256]{3,1,2,0:T(2,128)(2,1)}), bf16[64,2,18,256]{3,1,2,0:T(2,128)(2,1)S(1)}, u32[]{:S(2)}, u32[]{:S(2)}) %all-to-all-start) | async-done | bytes 1179680 | tf_op jit(solution)/shard_map/all_to_all | solution.py:68
  366.8 1.2 copy.26
  368.0 57.9 %all-gather.3.cloned.1.call-done = bf16[64,18,512]{2,1,0:T(8,128)(2,1)} async-done(((bf16[1,18,512]{2,1,0:T(8,128)(2,1)}), bf16[64,18,512]{2,1,0:T(8,128)(2,1)}) %all-gather.3.cloned.1.call-update) | async-done | bytes 1179664 | tf_op jit(solution)/shard_map/all_gather | solution.py:76
  425.9 3.1 reshape.33
  (1 shorter events, 0.0 us)
Async XLA Ops:
  7.2 211.4 %all-reduce.6.cloned.1.call-start = ((), (), s32[]{:S(2)}) async-start(), calls=%async_computation.4 | async-start | bytes 9437184
  9.6 7.7 %copy-start = (bf16[2,1152,512]{2,1,0:T(8,128)(2,1)S(1)}, bf16[2,1152,512]{2,1,0:T(8,128)(2,1)}, u32[]{:S(2)}) copy-start(bf16[2,1152,512]{2,1,0:T(8,128)(2,1)} %param.13) | copy-start | bytes 7077892
  19.2 0.7 copy-start.12
  19.2 200.8 %copy-start.8 = (bf16[2,2,256]{2,1,0:T(2,128)(2,1)S(1)}, bf16[2,2,256]{2,1,0:T(2,128)(2,1)}, u32[]{:S(2)}) copy-start(bf16[2,2,256]{2,1,0:T(2,128)(2,1)} %param.14) | copy-start | bytes 6148
  19.2 306.2 %copy-start.2 = (f32[2,18,256]{2,0,1:T(2,128)S(1)}, f32[2,18,256]{2,0,1:T(2,128)}, u32[]{:S(2)}) copy-start(f32[2,18,256]{2,0,1:T(2,128)} %param.15) | copy-start | bytes 110596
  19.2 306.2 %copy-start.3 = (f32[2,18,256]{2,0,1:T(2,128)S(1)}, f32[2,18,256]{2,0,1:T(2,128)}, u32[]{:S(2)}) copy-start(f32[2,18,256]{2,0,1:T(2,128)} %param.16) | copy-start | bytes 110596
  19.2 306.2 %copy-start.4 = (f32[2,18,256]{2,0,1:T(2,128)S(1)}, f32[2,18,256]{2,0,1:T(2,128)}, u32[]{:S(2)}) copy-start(f32[2,18,256]{2,0,1:T(2,128)} %param.17) | copy-start | bytes 110596
  19.3 317.0 %copy-start.5 = (f32[18,128]{1,0:T(8,128)S(1)}, f32[18,128]{1,0:T(8,128)}, u32[]{:S(2)}) copy-start(f32[18,128]{1,0:T(8,128)} %param.18) | copy-start | bytes 27652
  19.3 317.0 %copy-start.6 = (f32[18,128]{1,0:T(8,128)S(1)}, f32[18,128]{1,0:T(8,128)}, u32[]{:S(2)}) copy-start(f32[18,128]{1,0:T(8,128)} %param.19) | copy-start | bytes 27652
  19.3 317.0 %copy-start.7 = (f32[18,128]{1,0:T(8,128)S(1)}, f32[18,128]{1,0:T(8,128)}, u32[]{:S(2)}) copy-start(f32[18,128]{1,0:T(8,128)} %param.20) | copy-start | bytes 27652
  19.3 326.7 %copy-start.9 = (f32[2,256]{1,0:T(2,128)S(1)}, f32[2,256]{1,0:T(2,128)}, u32[]{:S(2)}) copy-start(f32[2,256]{1,0:T(2,128)} %param.21) | copy-start | bytes 6148
  19.3 326.7 %copy-start.10 = (f32[2,256]{1,0:T(2,128)S(1)}, f32[2,256]{1,0:T(2,128)}, u32[]{:S(2)}) copy-start(f32[2,256]{1,0:T(2,128)} %param.22) | copy-start | bytes 6148
  19.3 326.7 %copy-start.11 = (f32[2,256]{1,0:T(2,128)S(1)}, f32[2,256]{1,0:T(2,128)}, u32[]{:S(2)}) copy-start(f32[2,256]{1,0:T(2,128)} %param.23) | copy-start | bytes 6148
  19.3 223.4 %reduce-scatter.2.cloned.1.call-start = ((), (), s32[]{:S(2)}) async-start(), calls=%async_computation.2 | async-start | bytes 61440 | tf_op jit(solution)/shard_map/reduce_scatter | solution.py:50
  242.7 93.6 %copy-start.1 = (f32[18,128]{1,0:T(8,128)S(1)}, f32[18,128]{1,0:T(8,128)}, u32[]{:S(2)}) copy-start(f32[18,128]{1,0:T(8,128)} %reduce-scatter.2.cloned.1.call-done) | copy-start | bytes 27652
  328.6 38.2 %all-to-all-start = ((bf16[64,2,18,256]{3,1,2,0:T(2,128)(2,1)}), bf16[64,2,18,256]{3,1,2,0:T(2,128)(2,1)S(1)}, u32[]{:S(2)}, u32[]{:S(2)}) async-start(bf16[64,2,18,256]{3,1,2,0:T(2,128)(2,1)} %stack.2), calls=%async_computation.1 | async-start | bytes 2359296 | tf_op jit(solution)/shard_map/all_to_all | solution.py:68
  336.2 89.7 %all-gather.3.cloned.1.call-start = ((), (), s32[]{:S(2)}) async-start(), calls=%async_computation.3 | async-start | bytes 1597440 | tf_op jit(solution)/shard_map/all_gather | solution.py:76
Sparse Core Ops, SparseCore 0:
  19.4 199.1 all-reduce.5
  221.8 20.8 reduce-scatter.1
  346.1 79.7 all-gather.2
